TPU v7x, 32 devices: a whole 2x2x4 slice. The times are simulated.
32 devices in a mesh: chan: 8 (over z, y), win: 4 (over x, core).
Axes of the slice: x: 2, y: 2, z: 4, core: 2. Of those that a mesh axis runs over, the one named last changes fastest.
Arguments:
- samples: bfloat16 [8, 256, 6144], P('win', 'chan'), may hold values from -6 to 6
- pair_offsets: int32 [8, 3], P('chan'), may hold values from 0 to 2, each once within a row
- spectral_slot_position: int32 [1024], replicated, may hold values from 1 to 3071, as said below
Outputs:
- correlations: float32 [256, 3, 2, 32, 1024], P('chan', None, None, None, 'win')
Inputs may be any that keep to these rules, and one draw needn't show every extreme that they name: `pair_offsets`: each row holds every offset of 0 to 2 once. `spectral_slot_position`: distinct and rising; the first is 1 and the last is 3071.
All inputs are finite; a program needn't handle non-finite values.
Results may differ from a plain program's by a relative error of at most 0.0036.
Values sent between devices are 32-bit elements; how exact they have to be, the bound alone decides.
No kernel may reach another device: no remote copies, remote signals or barrier semaphores. Data moves between devices by JAX's collectives and lax.ppermute only.
A program may use at most 64 MiB of HBM per device.

v0:
```python
import math
import jax
import jax.numpy as jnp
from jax import lax
from jax.sharding import PartitionSpec as P

S = 6144
HALF = 64
TB = 1024
EPSILON = 1e-06


def passed_along(value, axis, steps):
    count = lax.axis_size(axis)
    leading, last = (max(0, -steps), min(count, count - steps))
    return lax.ppermute(value, axis, [(source, source + steps) for source in range(leading, last)])


def angle_parts(spectral_slot_position):
    factor = 2.0 * math.pi / S
    moments = jnp.arange(TB, dtype=jnp.int32)
    base = (moments[:, None] * spectral_slot_position[None, :] % S).astype(jnp.float32) * factor
    starts = jnp.arange(S // TB, dtype=jnp.int32) * TB
    turns = (starts[:, None] * spectral_slot_position[None, :] % S).astype(jnp.float32) * factor
    return (jnp.cos(base), jnp.sin(base), jnp.cos(turns), jnp.sin(turns))


def block_table(base_cos, base_sin, turn_cos, turn_sin):
    scale = 1.0 / math.sqrt(S)
    cos_part = (base_cos * turn_cos - base_sin * turn_sin) * scale
    sin_part = (base_sin * turn_cos + base_cos * turn_sin) * scale
    return jnp.concatenate([cos_part, sin_part], axis=-1).astype(jnp.bfloat16)


def whiten(spectra, half_width):
    freq_count = spectra.shape[-1]
    powers = spectra[..., 0, :] * spectra[..., 0, :] + spectra[..., 1, :] * spectra[..., 1, :]
    places = jnp.arange(freq_count, dtype=jnp.int32)
    banded = (jnp.abs(places[:, None] - places[None, :]) <= half_width).astype(jnp.float32)
    tallies = jnp.sum(banded, axis=0)
    flattened = powers.reshape(-1, freq_count)
    smoothed_amplitude = (
        jnp.dot(flattened, banded, precision=lax.Precision.HIGHEST).reshape(powers.shape) / tallies
    )
    amplitude = jnp.sqrt(smoothed_amplitude + EPSILON)
    return spectra / amplitude[..., None, :]


def arrange(field):
    win_count, chan_count, _, freq_count = field.shape
    return field.transpose(3, 1, 0, 2).reshape(freq_count, chan_count, win_count * 2)


def pair_blocks(spectra, offsets, windows):
    nearer = passed_along(spectra, "chan", 1)
    farther = passed_along(spectra, "chan", 2)
    win_count, chan_count, _, freq_count = spectra.shape
    flipped = jnp.stack([spectra[:, :, 1], -spectra[:, :, 0]], axis=2)
    left = jnp.concatenate([arrange(spectra), arrange(flipped)], axis=1)
    right = jnp.concatenate([arrange(spectra), arrange(nearer), arrange(farther)], axis=1)
    joined = jnp.einsum("fik,fjk->fij", left, right, precision=lax.Precision.HIGHEST) / windows
    joined = joined.reshape(freq_count, 2, chan_count, 3, chan_count)
    slots = []
    for position in range(offsets.shape[0]):
        chosen = offsets[position]
        slots.append(
            jnp.where(
                chosen == 0,
                joined[:, :, :, 0],
                jnp.where(chosen == 1, joined[:, :, :, 1], joined[:, :, :, 2]),
            )
        )
    stacked = jnp.stack(slots, axis=0)
    return stacked.transpose(3, 0, 2, 4, 1)


def shards(samples, pair_offsets, spectral_slot_position):
    win_count, sensor_total, segment_span = samples.shape
    freq_count = spectral_slot_position.shape[0]
    time_series = samples.reshape(win_count * sensor_total, segment_span)
    base_cos, base_sin, turn_cos, turn_sin = angle_parts(spectral_slot_position)

    def add_block(step, total):
        piece = lax.dynamic_slice_in_dim(time_series, step * TB, TB, 1)
        row_cos = lax.dynamic_slice_in_dim(turn_cos, step, 1, 0)
        row_sin = lax.dynamic_slice_in_dim(turn_sin, step, 1, 0)
        table = block_table(base_cos, base_sin, row_cos, row_sin)
        return total + jnp.dot(piece, table, preferred_element_type=jnp.float32)

    initial = jnp.zeros((win_count * sensor_total, 2 * freq_count), jnp.float32)
    raw_parts = lax.fori_loop(0, segment_span // TB, add_block, initial)
    spectra = jnp.stack([raw_parts[:, :freq_count], -raw_parts[:, freq_count:]], axis=1)
    spectra = spectra.reshape(win_count, sensor_total, 2, freq_count)
    whitened = whiten(spectra, HALF)
    offsets = pair_offsets[0]
    slabs = lax.all_to_all(whitened, "win", split_axis=3, concat_axis=0, tiled=True)
    return pair_blocks(slabs, offsets, slabs.shape[0])


def solution(mesh):
    in_specs = (P("win", "chan", None), P("chan", None), P())
    out_specs = P("chan", None, None, None, "win")
    return jax.shard_map(shards, mesh=mesh, in_specs=in_specs, out_specs=out_specs, check_vma=False)
```

profile of v0, /device:TPU:28, one launch (start us, length us, event | category | flops | bytes accessed | tf_op | source)
XLA Modules:
  0.0 227.4 jit_solution(14979115997876258393)
XLA Ops:
  0.0 0.2 convert_reduce_fusion
  0.2 0.9 fusion.59
  1.1 138.7 %while.16 = (s32[]{:T(128)}, f32[64,2048]{1,0:T(8,128)S(1)}, bf16[64,6144]{1,0:T(8,128)(2,1)}, f32[6,1024]{1,0:T(8,128)S(1)}, f32[6,1024]{1,0:T(8,128)S(1)}, /*i...) while((s32[]{:T(128)}, f32[64,2048]{1,0:T(8,128)S(1)}, ...), condition=%wide.region_1.2_spmd.clone.clone.clone, body=%wide.region_0.1_spmd.clone.clone.clone.sunk | while | flops 297009152 | bytes 9597093 | solution.py:91
  1.2 20.5 %fusion.73 = (bf16[1024,1024]{1,0:T(8,128)(2,1)S(1)}, bf16[1024,1024]{1,0:T(8,128)(2,1)}) fusion(s32[1024]{0:T(1024)} %get-tuple-element.293, f32[1024]{0:T(1024)S(1)} %bitcast.88, f32[1024]{0:T(1024)S(1)} %bitcast.89), kind=kLoop, calls=%fused_computation.20.clone.1 | loop fusion | flops 19922944 | bytes 4206592 | tf_op jit(solution)/shard_map/convert
  21.7 2.6 %fusion.74 = f32[64,2048]{1,0:T(8,128)S(1)} fusion(bf16[1024,1024]{1,0:T(8,128)(2,1)} %get-tuple-element.266, bf16[1024,1024]{1,0:T(8,128)(2,1)S(1)} %get-tuple-element.267, f32[64,2048]{1,0:T(8,128)S(1)} %get-tuple-element.279, pred[]{:T(512)S(6)} %compare.5, bf16[64,6144]{1,0:T(8,128)(2,1)} %get-tuple-element.290, s32[]{:T(128)S(6)} %select_n.219), kind=kOutput, calls=%fused_computation.25.clone.1 | convolution fusion | flops 277086208 | bytes 5373957 | tf_op jit(solution)/shard_map/while/body/eval_jaxpr/dot_general | solution.py:88
  24.3 20.5 %fusion.73 = (bf16[1024,1024]{1,0:T(8,128)(2,1)S(1)}, bf16[1024,1024]{1,0:T(8,128)(2,1)}) fusion(s32[1024]{0:T(1024)} %get-tuple-element.293, f32[1024]{0:T(1024)S(1)} %bitcast.88, f32[1024]{0:T(1024)S(1)} %bitcast.89), kind=kLoop, calls=%fused_computation.20.clone.1 | loop fusion | flops 19922944 | bytes 4206592 | tf_op jit(solution)/shard_map/convert
  44.8 2.6 %fusion.74 = f32[64,2048]{1,0:T(8,128)S(1)} fusion(bf16[1024,1024]{1,0:T(8,128)(2,1)} %get-tuple-element.266, bf16[1024,1024]{1,0:T(8,128)(2,1)S(1)} %get-tuple-element.267, f32[64,2048]{1,0:T(8,128)S(1)} %get-tuple-element.279, pred[]{:T(512)S(6)} %compare.5, bf16[64,6144]{1,0:T(8,128)(2,1)} %get-tuple-element.290, s32[]{:T(128)S(6)} %select_n.219), kind=kOutput, calls=%fused_computation.25.clone.1 | convolution fusion | flops 277086208 | bytes 5373957 | tf_op jit(solution)/shard_map/while/body/eval_jaxpr/dot_general | solution.py:88
  47.4 20.5 %fusion.73 = (bf16[1024,1024]{1,0:T(8,128)(2,1)S(1)}, bf16[1024,1024]{1,0:T(8,128)(2,1)}) fusion(s32[1024]{0:T(1024)} %get-tuple-element.293, f32[1024]{0:T(1024)S(1)} %bitcast.88, f32[1024]{0:T(1024)S(1)} %bitcast.89), kind=kLoop, calls=%fused_computation.20.clone.1 | loop fusion | flops 19922944 | bytes 4206592 | tf_op jit(solution)/shard_map/convert
  67.9 2.6 %fusion.74 = f32[64,2048]{1,0:T(8,128)S(1)} fusion(bf16[1024,1024]{1,0:T(8,128)(2,1)} %get-tuple-element.266, bf16[1024,1024]{1,0:T(8,128)(2,1)S(1)} %get-tuple-element.267, f32[64,2048]{1,0:T(8,128)S(1)} %get-tuple-element.279, pred[]{:T(512)S(6)} %compare.5, bf16[64,6144]{1,0:T(8,128)(2,1)} %get-tuple-element.290, s32[]{:T(128)S(6)} %select_n.219), kind=kOutput, calls=%fused_computation.25.clone.1 | convolution fusion | flops 277086208 | bytes 5373957 | tf_op jit(solution)/shard_map/while/body/eval_jaxpr/dot_general | solution.py:88
  70.5 20.5 %fusion.73 = (bf16[1024,1024]{1,0:T(8,128)(2,1)S(1)}, bf16[1024,1024]{1,0:T(8,128)(2,1)}) fusion(s32[1024]{0:T(1024)} %get-tuple-element.293, f32[1024]{0:T(1024)S(1)} %bitcast.88, f32[1024]{0:T(1024)S(1)} %bitcast.89), kind=kLoop, calls=%fused_computation.20.clone.1 | loop fusion | flops 19922944 | bytes 4206592 | tf_op jit(solution)/shard_map/convert
  91.0 2.6 %fusion.74 = f32[64,2048]{1,0:T(8,128)S(1)} fusion(bf16[1024,1024]{1,0:T(8,128)(2,1)} %get-tuple-element.266, bf16[1024,1024]{1,0:T(8,128)(2,1)S(1)} %get-tuple-element.267, f32[64,2048]{1,0:T(8,128)S(1)} %get-tuple-element.279, pred[]{:T(512)S(6)} %compare.5, bf16[64,6144]{1,0:T(8,128)(2,1)} %get-tuple-element.290, s32[]{:T(128)S(6)} %select_n.219), kind=kOutput, calls=%fused_computation.25.clone.1 | convolution fusion | flops 277086208 | bytes 5373957 | tf_op jit(solution)/shard_map/while/body/eval_jaxpr/dot_general | solution.py:88
  93.7 20.5 %fusion.73 = (bf16[1024,1024]{1,0:T(8,128)(2,1)S(1)}, bf16[1024,1024]{1,0:T(8,128)(2,1)}) fusion(s32[1024]{0:T(1024)} %get-tuple-element.293, f32[1024]{0:T(1024)S(1)} %bitcast.88, f32[1024]{0:T(1024)S(1)} %bitcast.89), kind=kLoop, calls=%fused_computation.20.clone.1 | loop fusion | flops 19922944 | bytes 4206592 | tf_op jit(solution)/shard_map/convert
  114.2 2.6 %fusion.74 = f32[64,2048]{1,0:T(8,128)S(1)} fusion(bf16[1024,1024]{1,0:T(8,128)(2,1)} %get-tuple-element.266, bf16[1024,1024]{1,0:T(8,128)(2,1)S(1)} %get-tuple-element.267, f32[64,2048]{1,0:T(8,128)S(1)} %get-tuple-element.279, pred[]{:T(512)S(6)} %compare.5, bf16[64,6144]{1,0:T(8,128)(2,1)} %get-tuple-element.290, s32[]{:T(128)S(6)} %select_n.219), kind=kOutput, calls=%fused_computation.25.clone.1 | convolution fusion | flops 277086208 | bytes 5373957 | tf_op jit(solution)/shard_map/while/body/eval_jaxpr/dot_general | solution.py:88
  116.8 20.5 %fusion.73 = (bf16[1024,1024]{1,0:T(8,128)(2,1)S(1)}, bf16[1024,1024]{1,0:T(8,128)(2,1)}) fusion(s32[1024]{0:T(1024)} %get-tuple-element.293, f32[1024]{0:T(1024)S(1)} %bitcast.88, f32[1024]{0:T(1024)S(1)} %bitcast.89), kind=kLoop, calls=%fused_computation.20.clone.1 | loop fusion | flops 19922944 | bytes 4206592 | tf_op jit(solution)/shard_map/convert
  137.3 2.6 %fusion.74 = f32[64,2048]{1,0:T(8,128)S(1)} fusion(bf16[1024,1024]{1,0:T(8,128)(2,1)} %get-tuple-element.266, bf16[1024,1024]{1,0:T(8,128)(2,1)S(1)} %get-tuple-element.267, f32[64,2048]{1,0:T(8,128)S(1)} %get-tuple-element.279, pred[]{:T(512)S(6)} %compare.5, bf16[64,6144]{1,0:T(8,128)(2,1)} %get-tuple-element.290, s32[]{:T(128)S(6)} %select_n.219), kind=kOutput, calls=%fused_computation.25.clone.1 | convolution fusion | flops 277086208 | bytes 5373957 | tf_op jit(solution)/shard_map/while/body/eval_jaxpr/dot_general | solution.py:88
  139.9 0.1 multiply_add_fusion
  140.0 0.9 fusion.52
  140.8 0.1 maximum_divide_fusion
  140.9 1.4 copy.35
  142.2 2.2 reshape.161
  144.5 0.0 copy-start.1
  144.5 11.4 %all_to_all.18 = f32[4,1,32768]{2,1,0:T(1,128)S(1)} all-to-all(f32[4,1,32768]{2,1,0:T(1,128)S(1)} %reshape.161), channel_id=1, replica_groups=mesh['chan'=8,'win'=4] {'win'}, dimensions={0} | all-to-all | bytes 1048576 | tf_op jit(solution)/shard_map/all_to_all | solution.py:96
  155.8 0.5 broadcast.93
  156.4 2.1 reduce
  158.5 1.8 reshape.162
  160.3 0.9 copy.36
  161.2 1.3 collective-permute-start
  162.5 1.5 collective-permute-start.1
  164.0 0.0 copy-done.1
  164.0 0.6 fusion.65
  168.4 2.3 copy.38
  170.6 1.5 copy.37
  172.1 4.4 %collective-permute-done = f32[8,32,2,256]{3,1,2,0:T(8,128)} collective-permute-done((f32[8,32,2,256]{3,1,2,0:T(8,128)S(1)}, f32[8,32,2,256]{3,1,2,0:T(8,128)}, u32[]{:S(2)}, u32[]{:S(2)}) %collective-permute-start) | collective-permute-done | bytes 524320 | tf_op jit(solution)/shard_map/ppermute | solution.py:16
  176.5 3.9 %copy.39 = f32[256,32,8,2]{1,3,2,0:T(2,128)} copy(f32[256,32,8,2]{0,1,3,2:T(8,128)} %bitcast.13) | data formatting | bytes 1048576 | tf_op jit(solution)/shard_map/transpose | solution.py:51
  180.4 7.1 %collective-permute-done.1 = f32[8,32,2,256]{3,1,2,0:T(8,128)S(1)} collective-permute-done((f32[8,32,2,256]{3,1,2,0:T(8,128)S(1)}, f32[8,32,2,256]{3,1,2,0:T(8,128)S(1)}, u32[]{:S(2)}, u32[]{:S(2)}) %collective-permute-start.1) | collective-permute-done | bytes 524320 | tf_op jit(solution)/shard_map/ppermute | solution.py:16
  187.6 2.4 %copy.40 = f32[256,32,8,2]{1,3,2,0:T(2,128)} copy(f32[256,32,8,2]{0,1,3,2:T(8,128)S(1)} %bitcast.87) | data formatting | bytes 1048576 | tf_op jit(solution)/shard_map/transpose | solution.py:51
  190.0 18.9 %broadcast_multiply_fusion = f32[256,64,96]{2,1,0:T(8,128)} fusion(f32[256,32,16]{1,2,0:T(8,128)} %bitcast.76, f32[256,32,16]{1,2,0:T(8,128)S(1)} %bitcast.75, f32[256,32,16]{1,2,0:T(8,128)} %bitcast.78, f32[256,32,16]{1,2,0:T(8,128)} %bitcast.77), kind=kOutput, calls=%fused_computation.32 | convolution fusion | flops 304611328 | bytes 8388608 | tf_op jit(solution)/shard_map/fik,fjk->fij/dot_general | solution.py:61
  208.9 8.5 %copy.41 = f32[256,64,96]{0,2,1:T(8,128)} copy(f32[256,64,96]{2,1,0:T(8,128)} %broadcast_multiply_fusion) | data formatting | bytes 12582912 | tf_op jit(solution)/shard_map/div | solution.py:61
  217.4 0.0 copy-start
  217.4 3.7 %select_bitcast_fusion = f32[1,256,2,32,32]{1,4,3,2,0:T(8,128)S(1)} fusion(f32[256,2,32,3,32]{0,4,3,2,1:T(8,128)} %bitcast.73, pred[]{:T(512)} %bitcast.27, pred[]{:T(512)} %bitcast.25), kind=kLoop, calls=%fused_computation.51 | loop fusion | flops 1048576 | bytes 8388610 | tf_op jit(solution)/shard_map/jit(_where)/select_n | solution.py:67
  221.2 0.9 copy-done
  222.1 0.7 fusion.42
  222.8 1.1 maximum_bitcast_fusion
  223.9 3.5 %copy.48 = f32[32,3,2,32,256]{4,3,2,1,0:T(8,128)} copy(f32[32,3,2,32,256]{4,3,0,2,1:T(8,128)S(1)} %maximum_bitcast_fusion) | data formatting | bytes 12582912 | tf_op jit(solution)/shard_map/transpose | solution.py:74
  (10 shorter events, 0.2 us)
Async XLA Ops:
  144.5 19.5 %copy-start.1 = (s32[1,3]{1,0:T(1,128)S(1)}, s32[1,3]{1,0:T(1,128)}, u32[]{:S(2)}) copy-start(s32[1,3]{1,0:T(1,128)} %param.6) | copy-start | bytes 40
  161.2 15.3 %collective-permute-start = (f32[8,32,2,256]{3,1,2,0:T(8,128)S(1)}, f32[8,32,2,256]{3,1,2,0:T(8,128)}, u32[]{:S(2)}, u32[]{:S(2)}) collective-permute-start(f32[8,32,2,256]{3,1,2,0:T(8,128)S(1)} %bitcast.81), channel_id=1, source_target_pairs={{0,4},{4,8},{8,12},{12,16},{16,20},{20,24},{24,28},{1,5},{5,9},{9,... | collective-permute-start | bytes 1572872 | tf_op jit(solution)/shard_map/ppermute | solution.py:16
  162.5 25.1 %collective-permute-start.1 = (f32[8,32,2,256]{3,1,2,0:T(8,128)S(1)}, f32[8,32,2,256]{3,1,2,0:T(8,128)S(1)}, u32[]{:S(2)}, u32[]{:S(2)}) collective-permute-start(f32[8,32,2,256]{3,1,2,0:T(8,128)S(1)} %bitcast.82), channel_id=1, source_target_pairs={{0,8},{4,12},{8,16},{12,20},{16,24},{20,28},{1,9},{5,13},{9,17},{1... | collective-permute-start | bytes 1572872 | tf_op jit(solution)/shard_map/ppermute | solution.py:16
  217.4 4.7 %copy-start = (f32[256,64,96]{0,2,1:T(8,128)S(1)}, f32[256,64,96]{0,2,1:T(8,128)}, u32[]{:S(2)}) copy-start(f32[256,64,96]{0,2,1:T(8,128)} %copy.41) | copy-start | bytes 18874372
where the time goes:
time: 228 us; the launch traced here: 227 us
  other arithmetic  132 us (58%)
  matrix products  35.3 us (15%)
  local copies, waits for them, and re-layouts  30.5 us (13%)
  waiting for transfers between devices  11.5 us (5%)
  blocking collectives  11.4 us (5%)
  between operations  3.83 us (2%)
  starting transfers between devices  2.76 us (1%)
    another operation x6, other arithmetic  123 us
    dot_general x1, matrix products, pair_blocks(): jnp.einsum('fik,fjk->fij', left, right, precision=lax.Precision.HIGHEST)  18.9 us
    dot_general x6, matrix products, add_block(): return total + jnp.dot(piece, table, preferred_element_type=jnp.float32)  15.5 us
    ppermute x2, waiting for transfers between devices, passed_along(): lax.ppermute(value, axis, [(source, source + steps) for source in range(l...  11.5 us
    all_to_all x1, blocking collectives, shards(): lax.all_to_all(whitened, 'win', split_axis=3, concat_axis=0, tiled=True)  11.4 us
    transpose x4, local copies, waits for them, and re-layouts, arrange(): field.transpose(3, 1, 0, 2).reshape(freq_count, chan_count, win_count * 2)  10.1 us
    div x1, local copies, waits for them, and re-layouts, pair_blocks(): jnp.einsum('fik,fjk->fij', left, right, precision=lax.Precision.HIGHEST)  8.54 us
    unnamed x6, local copies, waits for them, and re-layouts  4.95 us
  transfers between devices with their start and end apart: 2, of which 2 were waited for; matrix products, arithmetic and copies ran while one was open for 4% of the time, Pallas kernels for 0%

commit v1 on v0

--- a/solution.py
+++ b/solution.py
@@ -8,6 +8,18 @@
 HALF = 64
 TB = 1024
 EPSILON = 1e-06
+
+
+def cut_along(array, dim, count):
+    shape = array.shape
+    tiles = array.reshape(*shape[:dim], count, shape[dim] // count, *shape[dim + 1 :])
+    return jnp.moveaxis(tiles, dim, 0)
+
+
+def laid_out(parts, dim):
+    parts = jnp.moveaxis(parts, 0, dim)
+    shape = parts.shape
+    return parts.reshape(*shape[:dim], shape[dim] * shape[dim + 1], *shape[dim + 2 :])
 
 
 def passed_along(value, axis, steps):
@@ -93,7 +105,15 @@
     spectra = spectra.reshape(win_count, sensor_total, 2, freq_count)
     whitened = whiten(spectra, HALF)
     offsets = pair_offsets[0]
-    slabs = lax.all_to_all(whitened, "win", split_axis=3, concat_axis=0, tiled=True)
+    size, index = (lax.axis_size("win"), lax.axis_index("win"))
+    blocks = cut_along(whitened, 3, size)
+    out = blocks
+    for lap in range(1, size):
+        target, source_2 = ((index + lap) % size, (index - lap) % size)
+        sent = lax.dynamic_index_in_dim(blocks, target, 0)
+        theirs = lax.ppermute(sent, "win", [(i, (i + lap) % size) for i in range(size)])
+        out = lax.dynamic_update_slice_in_dim(out, theirs, source_2, axis=0)
+    slabs = laid_out(out, 0)
     return pair_blocks(slabs, offsets, slabs.shape[0])
 
 

time: 228 us -> 218 us (0.956)
  blocking collectives: 11.4 us -> 0 us
  local copies, waits for them, and re-layouts: 30.5 us -> 24.2 us
  waiting for transfers between devices: 11.5 us -> 17.2 us
  starting transfers between devices: 2.76 us -> 5.76 us
    all_to_all x1 -> x0, blocking collectives: 11.4 us -> none  [shards(): lax.all_to_all(whitened, 'win', split_axis=3, concat_axis=0, tiled=True)]
    ppermute x0 -> x3, waiting for transfers between devices: none -> 4.5 us  [shards(): lax.ppermute(sent, 'win', [(i, (i + lap) % size) for i in range(size)])]
    unnamed x6 -> x4, local copies, waits for them, and re-layouts: 4.95 us -> 0.93 us
    ppermute x0 -> x3, starting transfers between devices: none -> 3 us  [shards(): lax.ppermute(sent, 'win', [(i, (i + lap) % size) for i in range(size)])]
  transfers between devices with their start and end apart: 2 -> 5, of which waited for: 2 -> 5; matrix products, arithmetic and copies ran while one was open for 4% -> 4% of each run, Pallas kernels for 0% -> 0%
where the time goes in v1:
time: 218 us; the launch traced here: 217 us
  other arithmetic  130 us (60%)
  matrix products  35.3 us (16%)
  local copies, waits for them, and re-layouts  24.2 us (11%)
  waiting for transfers between devices  17.2 us (8%)
  starting transfers between devices  5.76 us (3%)
  between operations  4.02 us (2%)
    another operation x6, other arithmetic  123 us
    dot_general x1, matrix products, pair_blocks(): jnp.einsum('fik,fjk->fij', left, right, precision=lax.Precision.HIGHEST)  18.9 us
    dot_general x6, matrix products, add_block(): return total + jnp.dot(piece, table, preferred_element_type=jnp.float32)  15.5 us
    ppermute x2, waiting for transfers between devices, passed_along(): lax.ppermute(value, axis, [(source, source + steps) for source in range(l...  12.7 us
    transpose x4, local copies, waits for them, and re-layouts, arrange(): field.transpose(3, 1, 0, 2).reshape(freq_count, chan_count, win_count * 2)  10.1 us
    div x1, local copies, waits for them, and re-layouts, pair_blocks(): jnp.einsum('fik,fjk->fij', left, right, precision=lax.Precision.HIGHEST)  8.54 us
    ppermute x3, waiting for transfers between devices, shards(): lax.ppermute(sent, 'win', [(i, (i + lap) % size) for i in range(size)])  4.5 us
    select_n x2, other arithmetic, pair_blocks(): jnp.where(chosen == 0, joined[:, :, :, 0], jnp.where(chosen == 1, joined[...  4.45 us
  transfers between devices with their start and end apart: 5, of which 5 were waited for; matrix products, arithmetic and copies ran while one was open for 4% of the time, Pallas kernels for 0%

profile of v1, /device:TPU:28, one launch (start us, length us, event | category | flops | bytes accessed | tf_op | source)
XLA Modules:
  0.0 216.6 jit_solution(10973134920219353543)
XLA Ops:
  0.0 0.2 convert_reduce_fusion
  0.2 0.9 fusion.59
  1.1 138.7 %while.16 = (s32[]{:T(128)}, f32[64,2048]{1,0:T(8,128)S(1)}, bf16[64,6144]{1,0:T(8,128)(2,1)}, f32[6,1024]{1,0:T(8,128)S(1)}, f32[6,1024]{1,0:T(8,128)S(1)}, /*i...) while((s32[]{:T(128)}, f32[64,2048]{1,0:T(8,128)S(1)}, ...), condition=%wide.region_1.2_spmd.clone.clone.clone, body=%wide.region_0.1_spmd.clone.clone.clone.sunk | while | flops 297009152 | bytes 9597093 | solution.py:103
  1.2 20.5 %fusion.74 = (bf16[1024,1024]{1,0:T(8,128)(2,1)S(1)}, bf16[1024,1024]{1,0:T(8,128)(2,1)}) fusion(s32[1024]{0:T(1024)} %get-tuple-element.296, f32[1024]{0:T(1024)S(1)} %bitcast.91, f32[1024]{0:T(1024)S(1)} %bitcast.92), kind=kLoop, calls=%fused_computation.20.clone.1 | loop fusion | flops 19922944 | bytes 4206592 | tf_op jit(solution)/shard_map/convert
  21.7 2.6 %fusion.75 = f32[64,2048]{1,0:T(8,128)S(1)} fusion(bf16[1024,1024]{1,0:T(8,128)(2,1)} %get-tuple-element.269, bf16[1024,1024]{1,0:T(8,128)(2,1)S(1)} %get-tuple-element.270, f32[64,2048]{1,0:T(8,128)S(1)} %get-tuple-element.282, pred[]{:T(512)S(6)} %compare.11, bf16[64,6144]{1,0:T(8,128)(2,1)} %get-tuple-element.293, s32[]{:T(128)S(6)} %select_n.276), kind=kOutput, calls=%fused_computation.25.clone.1 | convolution fusion | flops 277086208 | bytes 5373957 | tf_op jit(solution)/shard_map/while/body/eval_jaxpr/dot_general | solution.py:100
  24.3 20.5 %fusion.74 = (bf16[1024,1024]{1,0:T(8,128)(2,1)S(1)}, bf16[1024,1024]{1,0:T(8,128)(2,1)}) fusion(s32[1024]{0:T(1024)} %get-tuple-element.296, f32[1024]{0:T(1024)S(1)} %bitcast.91, f32[1024]{0:T(1024)S(1)} %bitcast.92), kind=kLoop, calls=%fused_computation.20.clone.1 | loop fusion | flops 19922944 | bytes 4206592 | tf_op jit(solution)/shard_map/convert
  44.8 2.6 %fusion.75 = f32[64,2048]{1,0:T(8,128)S(1)} fusion(bf16[1024,1024]{1,0:T(8,128)(2,1)} %get-tuple-element.269, bf16[1024,1024]{1,0:T(8,128)(2,1)S(1)} %get-tuple-element.270, f32[64,2048]{1,0:T(8,128)S(1)} %get-tuple-element.282, pred[]{:T(512)S(6)} %compare.11, bf16[64,6144]{1,0:T(8,128)(2,1)} %get-tuple-element.293, s32[]{:T(128)S(6)} %select_n.276), kind=kOutput, calls=%fused_computation.25.clone.1 | convolution fusion | flops 277086208 | bytes 5373957 | tf_op jit(solution)/shard_map/while/body/eval_jaxpr/dot_general | solution.py:100
  47.4 20.5 %fusion.74 = (bf16[1024,1024]{1,0:T(8,128)(2,1)S(1)}, bf16[1024,1024]{1,0:T(8,128)(2,1)}) fusion(s32[1024]{0:T(1024)} %get-tuple-element.296, f32[1024]{0:T(1024)S(1)} %bitcast.91, f32[1024]{0:T(1024)S(1)} %bitcast.92), kind=kLoop, calls=%fused_computation.20.clone.1 | loop fusion | flops 19922944 | bytes 4206592 | tf_op jit(solution)/shard_map/convert
  67.9 2.6 %fusion.75 = f32[64,2048]{1,0:T(8,128)S(1)} fusion(bf16[1024,1024]{1,0:T(8,128)(2,1)} %get-tuple-element.269, bf16[1024,1024]{1,0:T(8,128)(2,1)S(1)} %get-tuple-element.270, f32[64,2048]{1,0:T(8,128)S(1)} %get-tuple-element.282, pred[]{:T(512)S(6)} %compare.11, bf16[64,6144]{1,0:T(8,128)(2,1)} %get-tuple-element.293, s32[]{:T(128)S(6)} %select_n.276), kind=kOutput, calls=%fused_computation.25.clone.1 | convolution fusion | flops 277086208 | bytes 5373957 | tf_op jit(solution)/shard_map/while/body/eval_jaxpr/dot_general | solution.py:100
  70.6 20.5 %fusion.74 = (bf16[1024,1024]{1,0:T(8,128)(2,1)S(1)}, bf16[1024,1024]{1,0:T(8,128)(2,1)}) fusion(s32[1024]{0:T(1024)} %get-tuple-element.296, f32[1024]{0:T(1024)S(1)} %bitcast.91, f32[1024]{0:T(1024)S(1)} %bitcast.92), kind=kLoop, calls=%fused_computation.20.clone.1 | loop fusion | flops 19922944 | bytes 4206592 | tf_op jit(solution)/shard_map/convert
  91.0 2.6 %fusion.75 = f32[64,2048]{1,0:T(8,128)S(1)} fusion(bf16[1024,1024]{1,0:T(8,128)(2,1)} %get-tuple-element.269, bf16[1024,1024]{1,0:T(8,128)(2,1)S(1)} %get-tuple-element.270, f32[64,2048]{1,0:T(8,128)S(1)} %get-tuple-element.282, pred[]{:T(512)S(6)} %compare.11, bf16[64,6144]{1,0:T(8,128)(2,1)} %get-tuple-element.293, s32[]{:T(128)S(6)} %select_n.276), kind=kOutput, calls=%fused_computation.25.clone.1 | convolution fusion | flops 277086208 | bytes 5373957 | tf_op jit(solution)/shard_map/while/body/eval_jaxpr/dot_general | solution.py:100
  93.7 20.5 %fusion.74 = (bf16[1024,1024]{1,0:T(8,128)(2,1)S(1)}, bf16[1024,1024]{1,0:T(8,128)(2,1)}) fusion(s32[1024]{0:T(1024)} %get-tuple-element.296, f32[1024]{0:T(1024)S(1)} %bitcast.91, f32[1024]{0:T(1024)S(1)} %bitcast.92), kind=kLoop, calls=%fused_computation.20.clone.1 | loop fusion | flops 19922944 | bytes 4206592 | tf_op jit(solution)/shard_map/convert
  114.2 2.6 %fusion.75 = f32[64,2048]{1,0:T(8,128)S(1)} fusion(bf16[1024,1024]{1,0:T(8,128)(2,1)} %get-tuple-element.269, bf16[1024,1024]{1,0:T(8,128)(2,1)S(1)} %get-tuple-element.270, f32[64,2048]{1,0:T(8,128)S(1)} %get-tuple-element.282, pred[]{:T(512)S(6)} %compare.11, bf16[64,6144]{1,0:T(8,128)(2,1)} %get-tuple-element.293, s32[]{:T(128)S(6)} %select_n.276), kind=kOutput, calls=%fused_computation.25.clone.1 | convolution fusion | flops 277086208 | bytes 5373957 | tf_op jit(solution)/shard_map/while/body/eval_jaxpr/dot_general | solution.py:100
  116.8 20.5 %fusion.74 = (bf16[1024,1024]{1,0:T(8,128)(2,1)S(1)}, bf16[1024,1024]{1,0:T(8,128)(2,1)}) fusion(s32[1024]{0:T(1024)} %get-tuple-element.296, f32[1024]{0:T(1024)S(1)} %bitcast.91, f32[1024]{0:T(1024)S(1)} %bitcast.92), kind=kLoop, calls=%fused_computation.20.clone.1 | loop fusion | flops 19922944 | bytes 4206592 | tf_op jit(solution)/shard_map/convert
  137.3 2.6 %fusion.75 = f32[64,2048]{1,0:T(8,128)S(1)} fusion(bf16[1024,1024]{1,0:T(8,128)(2,1)} %get-tuple-element.269, bf16[1024,1024]{1,0:T(8,128)(2,1)S(1)} %get-tuple-element.270, f32[64,2048]{1,0:T(8,128)S(1)} %get-tuple-element.282, pred[]{:T(512)S(6)} %compare.11, bf16[64,6144]{1,0:T(8,128)(2,1)} %get-tuple-element.293, s32[]{:T(128)S(6)} %select_n.276), kind=kOutput, calls=%fused_computation.25.clone.1 | convolution fusion | flops 277086208 | bytes 5373957 | tf_op jit(solution)/shard_map/while/body/eval_jaxpr/dot_general | solution.py:100
  139.9 0.1 multiply_add_fusion
  140.0 0.9 fusion.52
  140.8 0.0 copy-start.1
  140.9 0.1 stack.19
  141.0 0.1 copy.19
  141.1 0.1 stack.20
  141.2 0.1 copy.20
  141.3 0.1 maximum_divide_fusion
  141.4 0.1 collective-permute-start
  141.4 1.6 collective-permute-start.1
  143.0 1.4 collective-permute-start.2
  144.4 0.1 fusion.67
  144.5 2.1 collective-permute-done
  146.6 1.3 collective-permute-done.1
  147.9 1.1 collective-permute-done.2
  149.1 1.3 collective-permute-start.3
  150.4 1.5 collective-permute-start.4
  151.8 0.0 copy-done.1
  151.8 0.6 fusion.65
  156.3 2.3 %copy.23 = f32[256,32,8,2]{1,3,2,0:T(2,128)} copy(f32[256,32,8,2]{0,1,3,2:T(8,128)S(1)} %maximum_bitcast_fusion.1) | data formatting | bytes 1048576 | tf_op jit(solution)/shard_map/transpose | solution.py:63
  158.6 1.5 copy.22
  160.1 5.6 %collective-permute-done.3 = f32[8,32,2,256]{3,1,2,0:T(8,128)} collective-permute-done((f32[8,32,2,256]{3,1,2,0:T(8,128)S(1)}, f32[8,32,2,256]{3,1,2,0:T(8,128)}, u32[]{:S(2)}, u32[]{:S(2)}) %collective-permute-start.3) | collective-permute-done | bytes 524320 | tf_op jit(solution)/shard_map/ppermute | solution.py:28
  165.7 3.9 %copy.24 = f32[256,32,8,2]{1,3,2,0:T(2,128)} copy(f32[256,32,8,2]{0,1,3,2:T(8,128)} %bitcast.13) | data formatting | bytes 1048576 | tf_op jit(solution)/shard_map/transpose | solution.py:63
  169.6 7.1 %collective-permute-done.4 = f32[8,32,2,256]{3,1,2,0:T(8,128)S(1)} collective-permute-done((f32[8,32,2,256]{3,1,2,0:T(8,128)S(1)}, f32[8,32,2,256]{3,1,2,0:T(8,128)S(1)}, u32[]{:S(2)}, u32[]{:S(2)}) %collective-permute-start.4) | collective-permute-done | bytes 524320 | tf_op jit(solution)/shard_map/ppermute | solution.py:28
  176.8 2.4 %copy.25 = f32[256,32,8,2]{1,3,2,0:T(2,128)} copy(f32[256,32,8,2]{0,1,3,2:T(8,128)S(1)} %bitcast.90) | data formatting | bytes 1048576 | tf_op jit(solution)/shard_map/transpose | solution.py:63
  179.1 18.9 %broadcast_multiply_fusion = f32[256,64,96]{2,1,0:T(8,128)} fusion(f32[256,32,16]{1,2,0:T(8,128)} %bitcast.81, f32[256,32,16]{1,2,0:T(8,128)S(1)} %bitcast.80, f32[256,32,16]{1,2,0:T(8,128)} %bitcast.83, f32[256,32,16]{1,2,0:T(8,128)} %bitcast.82), kind=kOutput, calls=%fused_computation.32 | convolution fusion | flops 304611328 | bytes 8388608 | tf_op jit(solution)/shard_map/fik,fjk->fij/dot_general | solution.py:73
  198.1 8.5 %copy.26 = f32[256,64,96]{0,2,1:T(8,128)} copy(f32[256,64,96]{2,1,0:T(8,128)} %broadcast_multiply_fusion) | data formatting | bytes 12582912 | tf_op jit(solution)/shard_map/div | solution.py:73
  206.6 0.0 copy-start
  206.6 3.7 %select_bitcast_fusion = f32[1,256,2,32,32]{1,4,3,2,0:T(8,128)S(1)} fusion(f32[256,2,32,3,32]{0,4,3,2,1:T(8,128)} %bitcast.78, pred[]{:T(512)} %bitcast.27, pred[]{:T(512)} %bitcast.25), kind=kLoop, calls=%fused_computation.51 | loop fusion | flops 1048576 | bytes 8388610 | tf_op jit(solution)/shard_map/jit(_where)/select_n | solution.py:79
  210.4 0.9 copy-done
  211.3 0.7 fusion.42
  212.0 1.1 maximum_bitcast_fusion
  213.1 3.5 %copy.33 = f32[32,3,2,32,256]{4,3,2,1,0:T(8,128)} copy(f32[32,3,2,32,256]{4,3,0,2,1:T(8,128)S(1)} %maximum_bitcast_fusion) | data formatting | bytes 12582912 | tf_op jit(solution)/shard_map/transpose | solution.py:86
  (15 shorter events, 0.3 us)
Async XLA Ops:
  140.8 11.0 %copy-start.1 = (s32[1,3]{1,0:T(1,128)S(1)}, s32[1,3]{1,0:T(1,128)}, u32[]{:S(2)}) copy-start(s32[1,3]{1,0:T(1,128)} %param.6) | copy-start | bytes 40
  141.4 5.2 %collective-permute-start = (f32[1,2,32,2,256]{4,2,3,1,0:T(8,128)S(1)}, f32[1,2,32,2,256]{4,2,3,1,0:T(8,128)S(1)}, u32[]{:S(2)}, u32[]{:S(2)}) collective-permute-start(f32[1,2,32,2,256]{4,2,3,1,0:T(8,128)S(1)} %get-tuple-element.217), channel_id=1, source_target_pairs={{0,1},{1,2},{2,3},{3,0},{4,5},{5,6},{6,7},{7,4},{8,9},{9,10},{10,1... | collective-permute-start | bytes 393224 | tf_op jit(solution)/shard_map/ppermute | solution.py:114
  141.4 6.4 %collective-permute-start.1 = (f32[1,2,32,2,256]{4,2,3,1,0:T(8,128)S(1)}, f32[1,2,32,2,256]{4,2,3,1,0:T(8,128)S(1)}, u32[]{:S(2)}, u32[]{:S(2)}) collective-permute-start(f32[1,2,32,2,256]{4,2,3,1,0:T(8,128)S(1)} %get-tuple-element.216), channel_id=1, source_target_pairs={{0,2},{1,3},{2,0},{3,1},{4,6},{5,7},{6,4},{7,5},{8,10},{9,11},{10,... | collective-permute-start | bytes 393224 | tf_op jit(solution)/shard_map/ppermute | solution.py:114
  143.0 6.0 %collective-permute-start.2 = (f32[1,2,32,2,256]{4,2,3,1,0:T(8,128)S(1)}, f32[1,2,32,2,256]{4,2,3,1,0:T(8,128)S(1)}, u32[]{:S(2)}, u32[]{:S(2)}) collective-permute-start(f32[1,2,32,2,256]{4,2,3,1,0:T(8,128)S(1)} %get-tuple-element.215), channel_id=1, source_target_pairs={{0,3},{1,0},{2,1},{3,2},{4,7},{5,4},{6,5},{7,6},{8,11},{9,8},{10,9... | collective-permute-start | bytes 393224 | tf_op jit(solution)/shard_map/ppermute | solution.py:114
  149.1 16.6 %collective-permute-start.3 = (f32[8,32,2,256]{3,1,2,0:T(8,128)S(1)}, f32[8,32,2,256]{3,1,2,0:T(8,128)}, u32[]{:S(2)}, u32[]{:S(2)}) collective-permute-start(f32[8,32,2,256]{3,1,2,0:T(8,128)S(1)} %bitcast.84), channel_id=1, source_target_pairs={{0,4},{4,8},{8,12},{12,16},{16,20},{20,24},{24,28},{1,5},{5,9},{9,... | collective-permute-start | bytes 1572872 | tf_op jit(solution)/shard_map/ppermute | solution.py:28
  150.4 26.4 %collective-permute-start.4 = (f32[8,32,2,256]{3,1,2,0:T(8,128)S(1)}, f32[8,32,2,256]{3,1,2,0:T(8,128)S(1)}, u32[]{:S(2)}, u32[]{:S(2)}) collective-permute-start(f32[8,32,2,256]{3,1,2,0:T(8,128)S(1)} %bitcast.85), channel_id=1, source_target_pairs={{0,8},{4,12},{8,16},{12,20},{16,24},{20,28},{1,9},{5,13},{9,17},{1... | collective-permute-start | bytes 1572872 | tf_op jit(solution)/shard_map/ppermute | solution.py:28
  206.6 4.7 %copy-start = (f32[256,64,96]{0,2,1:T(8,128)S(1)}, f32[256,64,96]{0,2,1:T(8,128)}, u32[]{:S(2)}) copy-start(f32[256,64,96]{0,2,1:T(8,128)} %copy.26) | copy-start | bytes 18874372
